TPU v7x, 32 devices: a whole 2x2x4 slice. The times are simulated.
32 devices in a mesh: prow: 4 (over x, core), pcol: 8 (over z, y).
Axes of the slice: x: 2, y: 2, z: 4, core: 2. Of those that a mesh axis runs over, the one named last changes fastest.
Arguments:
- child_u: bfloat16 [2, 10, 4, 2, 8, 512, 128], P(None, None, 'prow', None, 'pcol'), may hold values from -5 to 5
- child_v: bfloat16 [2, 10, 4, 2, 8, 512, 128], P(None, None, 'prow', None, 'pcol'), may hold values from -5 to 5
- child_rank: int32 [2, 10, 4, 2, 8], P(None, None, 'prow', None, 'pcol'), may hold values from 0 to 128, as said below
- diag_shift: float32 [16, 512], replicated, may hold values from 0.5 to 4
Outputs:
- front_out: float32 [10, 4, 512, 2, 8, 512], P(None, 'prow', None, None, 'pcol')
Inputs may be any that keep to these rules, and one draw needn't show every extreme that they name: `child_rank`: 0 on and above the block diagonal (i <= j); below it 0 where the child has no tile, else from 16 to 128.
All inputs are finite; a program needn't handle non-finite values.
Results may differ from a plain program's by a relative error of at most 0.0003.
Values may be sent and summed in bfloat16 or wider, within the bound.
A program may use at most 320 MiB of HBM per device.

v0:
```python
import jax
import jax.numpy as jnp
from jax import lax
from jax.sharding import PartitionSpec as P

PANELS = 2


def spread(value, axis, root):
    mine = lax.axis_index(axis) == root
    return lax.psum(jnp.where(mine, value, jnp.zeros_like(value)), axis)


def factor_panel(column, panel_index, block_rows, block_cols, own_column, prow_count, pcol_count):
    extent = column.shape[-1]
    pivot_tile = spread(column[panel_index // prow_count], "prow", panel_index % prow_count)
    is_owner = own_column == panel_index % pcol_count
    pivot_tile = jnp.where(is_owner, pivot_tile, jnp.eye(extent, dtype=jnp.float32))
    factor = jnp.linalg.cholesky(pivot_tile)
    solved = lax.linalg.triangular_solve(
        factor, column.reshape(-1, extent), left_side=False, lower=True, transpose_a=True
    ).reshape(column.shape)
    below_mask = (block_rows > panel_index)[:, None, None]
    solved = jnp.where(below_mask, solved, 0.0)
    pivot_diag = jnp.diagonal(factor)
    at_pivot = (block_rows == panel_index)[:, None, None]
    panel_out = jnp.where(
        at_pivot, (factor * pivot_diag[None, :])[None], solved * pivot_diag[None, None, :]
    )
    rounded = solved.astype(jnp.bfloat16)
    received = spread(rounded, "pcol", panel_index % pcol_count)
    picked = jnp.take(received, block_cols // prow_count, axis=0)
    column_rows = spread(picked, "prow", own_column % prow_count)
    return (received, column_rows, panel_out, is_owner)


def trailing(column, received, other_rows):
    return column - jnp.einsum(
        "rab,cb->rac", received, other_rows, preferred_element_type=jnp.float32
    )


def on_device(child_u, child_v, child_rank, diag_shift):
    prow_count = lax.axis_size("prow")
    pcol_count = lax.axis_size("pcol")
    own_row = lax.axis_index("prow")
    own_column = lax.axis_index("pcol")
    rank_grid = child_rank[:, :, 0, :, 0]
    rows_here = rank_grid.shape[1]
    cols_here = rank_grid.shape[2]
    extent = child_u.shape[-2]
    keep_mask = (
        jnp.arange(child_u.shape[-1], dtype=jnp.int32)[None, None, None, :]
        < rank_grid[:, :, :, None]
    ).astype(jnp.bfloat16)
    left_factor = child_u[:, :, 0, :, 0] * keep_mask[:, :, :, None, :]
    right_factor = child_v[:, :, 0, :, 0] * keep_mask[:, :, :, None, :]
    tile_grid = jnp.einsum(
        "crtak,crtbk->rtab", left_factor, right_factor, preferred_element_type=jnp.float32
    )
    row_terms = jnp.einsum(
        "crtak,crtbk->rab", left_factor, left_factor, preferred_element_type=jnp.float32
    )
    column_terms = jnp.einsum(
        "crtak,crtbk->tab", right_factor, right_factor, preferred_element_type=jnp.float32
    )
    kept_rows = cols_here * pcol_count // prow_count
    partial_rows = lax.psum(row_terms[:kept_rows], "pcol")
    spare_rows = jnp.zeros((rows_here - kept_rows, extent, extent), jnp.float32)
    row_sums = jnp.concatenate([partial_rows, spare_rows], axis=0)
    column_sums = lax.psum(column_terms, "prow")
    block_rows = jnp.arange(rows_here, dtype=jnp.int32) * prow_count + own_row
    block_cols = jnp.arange(cols_here, dtype=jnp.int32) * pcol_count + own_column
    slab_total = diag_shift.shape[0]
    select_cols = (block_cols[:, None] == jnp.arange(slab_total, dtype=jnp.int32)[None, :]).astype(
        jnp.float32
    )
    shift_cols = jnp.dot(select_cols, diag_shift, precision=lax.Precision.HIGHEST)
    identity = jnp.eye(extent, dtype=jnp.float32)
    diag_terms = (
        row_sums[:, None]
        + column_sums[None, :]
        + identity[None, None] * shift_cols[None, :, None, :]
    )
    on_diagonal = (block_rows[:, None] == block_cols[None, :])[:, :, None, None]
    tile_grid = tile_grid + jnp.where(on_diagonal, diag_terms, 0.0)
    columns = [tile_grid[:, column_index] for column_index in range(cols_here)]
    results = [jnp.zeros_like(columns[0]) for column_index in range(cols_here)]
    for panel_index in range(PANELS):
        local_col = panel_index // pcol_count
        received, column_rows, panel_out, is_owner = factor_panel(
            columns[local_col],
            panel_index,
            block_rows,
            block_cols,
            own_column,
            prow_count,
            pcol_count,
        )
        results[local_col] = jnp.where(is_owner, panel_out, results[local_col])
        columns = [
            trailing(columns[column_index], received, column_rows[column_index])
            for column_index in range(cols_here)
        ]
    outputs = []
    for column_index in range(cols_here):
        lower_mask = (block_rows >= block_cols[column_index])[:, None, None]
        finished = jnp.where(lower_mask, columns[column_index], 0.0)
        outputs.append(
            jnp.where(block_cols[column_index] < PANELS, results[column_index], finished)
        )
    stacked = jnp.stack(outputs, axis=1)
    return stacked.transpose(0, 2, 1, 3)[:, None, :, :, None, :]


def solution(mesh):
    placed = (
        P(None, None, "prow", None, "pcol", None, None),
        P(None, None, "prow", None, "pcol", None, None),
        P(None, None, "prow", None, "pcol"),
        P(),
    )
    return jax.shard_map(
        on_device,
        mesh=mesh,
        in_specs=placed,
        out_specs=P(None, "prow", None, None, "pcol", None),
        check_vma=False,
    )
```

profile of v0, /device:TPU:0, one launch (start us, length us, event | category | flops | bytes accessed | tf_op | source)
XLA Modules:
  0.0 1351.2 jit_solution(12334410048220816827)
XLA Ops:
  36.5 14.6 %convolution_bitcast_fusion = f32[10,2,512,512]{2,3,0,1:T(8,128)} fusion(bf16[2,10,2,512,128]{4,3,2,1,0:T(8,128)(2,1)} %get-tuple-element.69, bf16[2,10,2,512,128]{4,3,2,1,0:T(8,128)(2,1)} %get-tuple-element.68), kind=kOutput, calls=%fused_computation.35 | convolution fusion | flops 2684354560 | bytes 31457280 | tf_op jit(solution)/shard_map/crtak,crtbk->rtab/dot_general | solution.py:58
  51.1 27.6 %all-reduce.13.cloned.1.call-done = f32[2,512,512]{2,1,0:T(8,128)} async-done(((f32[2,512,512]{2,1,0:T(8,128)}), f32[2,512,512]{2,1,0:T(8,128)}) %all-reduce.13.cloned.1.call-update) | async-done | bytes 2097168 | tf_op jit(solution)/shard_map/psum | solution.py:71
  81.6 157.3 %all-reduce.11.cloned.1.call-done = f32[4,512,512]{2,1,0:T(8,128)} async-done(((f32[4,512,512]{2,1,0:T(8,128)}), f32[4,512,512]{2,1,0:T(8,128)}) %all-reduce.11.cloned.1.call-update) | async-done | bytes 4194320 | tf_op jit(solution)/shard_map/psum | solution.py:68
  251.6 12.6 copy_add_fusion
  282.1 11.7 copy.45
  293.7 14.7 %all-reduce.15.cloned.1.call-done = f32[512,512]{0,1:T(8,128)} async-done(((f32[512,512]{0,1:T(8,128)}), f32[512,512]{0,1:T(8,128)}) %all-reduce.15.cloned.1.call-update) | async-done | bytes 1048592 | tf_op jit(solution)/shard_map/psum | solution.py:11
  311.6 11.7 cholesky.286
  333.9 11.7 cholesky.305
  356.3 11.7 cholesky.326
  379.2 11.7 cholesky.343
  397.9 11.7 while.4
  409.7 39.9 %custom-call.34 = f32[4,128,128]{1,2,0:T(8,128)} custom-call(f32[4,128,128]{2,1,0:T(8,128)S(1)} %get-tuple-element.22), custom_call_target="InvertDiagBlocksLowerTriangular" | custom-call | tf_op jit(solution)/shard_map/triangular_solve/custom-call.3 | solution.py:20
  475.4 14.6 %fusion.20 = f32[5120,128]{1,0:T(8,128)S(1)} fusion(f32[5120,128]{0,1:T(8,128)S(1)} %fusion.71, f32[5120,128]{0,1:T(8,128)S(1)} %fusion.72, f32[5120,128]{0,1:T(8,128)S(1)} %bitcast.181, f32[5120,512]{1,0:T(8,128)S(1)} %bitcast.191, f32[512,512]{1,0:T(8,128)} %get-tuple-element.198), kind=kOutput, calls=%fused_computation.41 | convolution fusion | flops 3024486400 | bytes 13303808 | tf_op jit(solution)/shard_map/triangular_solve/dot.12 | solution.py:20
  497.1 11.4 copy.46
  527.8 181.8 %all-reduce.17.cloned.1.call-done = bf16[10,512,512]{1,2,0:T(8,128)(2,1)} async-done(((bf16[10,512,512]{1,2,0:T(8,128)(2,1)}), bf16[10,512,512]{1,2,0:T(8,128)(2,1)}) %all-reduce.17.cloned.1.call-update) | async-done | bytes 5242896 | tf_op jit(solution)/shard_map/psum | solution.py:11
  714.1 35.4 %all-reduce.19.cloned.1.call-done = bf16[2,512,512]{1,2,0:T(8,128)(2,1)} async-done(((bf16[2,512,512]{1,2,0:T(8,128)(2,1)}), bf16[2,512,512]{1,2,0:T(8,128)(2,1)}) %all-reduce.19.cloned.1.call-update) | async-done | bytes 1048592 | tf_op jit(solution)/shard_map/psum | solution.py:11
  764.4 11.4 copy.53
  775.8 25.4 %all-reduce.21.cloned.1.call-done = f32[512,512]{0,1:T(8,128)} async-done(((f32[512,512]{0,1:T(8,128)}), f32[512,512]{0,1:T(8,128)}) %all-reduce.21.cloned.1.call-update) | async-done | bytes 1048592 | tf_op jit(solution)/shard_map/psum | solution.py:11
  802.9 11.7 cholesky.358
  827.2 11.7 cholesky.377
  852.0 11.7 cholesky.398
  875.7 11.7 cholesky.415
  894.0 11.8 while.5
  905.8 39.9 %custom-call.38 = f32[4,128,128]{1,2,0:T(8,128)} custom-call(f32[4,128,128]{2,1,0:T(8,128)S(1)} %get-tuple-element.23), custom_call_target="InvertDiagBlocksLowerTriangular" | custom-call | tf_op jit(solution)/shard_map/triangular_solve/custom-call.3 | solution.py:20
  971.8 14.4 %fusion.17 = f32[5120,128]{1,0:T(8,128)S(1)} fusion(f32[5120,128]{0,1:T(8,128)S(1)} %fusion.65, f32[5120,128]{0,1:T(8,128)S(1)} %fusion.66, f32[5120,128]{0,1:T(8,128)S(1)} %bitcast.184, f32[5120,512]{1,0:T(8,128)S(1)} %bitcast.197, f32[512,512]{1,0:T(8,128)} %get-tuple-element.197), kind=kOutput, calls=%fused_computation.40 | convolution fusion | flops 3024486400 | bytes 13303808 | tf_op jit(solution)/shard_map/triangular_solve/dot.12 | solution.py:20
  1004.6 11.5 copy.55
  1032.1 176.3 %all-reduce.23.cloned.1.call-done = bf16[10,512,512]{1,2,0:T(8,128)(2,1)} async-done(((bf16[10,512,512]{1,2,0:T(8,128)(2,1)}), bf16[10,512,512]{1,2,0:T(8,128)(2,1)}) %all-reduce.23.cloned.1.call-update) | async-done | bytes 5242896 | tf_op jit(solution)/shard_map/psum | solution.py:11
  1226.0 22.1 %all-reduce.25.cloned.1.call-done = bf16[2,512,512]{1,2,0:T(8,128)(2,1)} async-done(((bf16[2,512,512]{1,2,0:T(8,128)(2,1)}), bf16[2,512,512]{1,2,0:T(8,128)(2,1)}) %all-reduce.25.cloned.1.call-update) | async-done | bytes 1048592 | tf_op jit(solution)/shard_map/psum | solution.py:11
  1248.0 18.4 %fusion.4 = f32[10,1,512,512]{2,3,0,1:T(8,128)} fusion(f32[10,512,512]{1,2,0:T(8,128)} %fusion.47, f32[10,2,512,512]{2,3,1,0:T(8,128)} %copy-done.2, pred[10]{0:T(512)(128)(4,1)S(1)} %get-tuple-element.76, pred[]{:T(512)S(6)} %lt.48, bf16[10,512,512]{1,2,0:T(8,128)(2,1)} %all-reduce.23.cloned.1.call-done, bf16[2,512,512]{1,2,0:T(8,128)(2,1)} %all-reduce.25.cloned.1.call-done), kind=kOutput, calls=%fused_computation.15 | convolution fusion | flops 2694840320 | bytes 37224460 | tf_op jit(solution)/shard_map/rab,cb->rac/dot_general | solution.py:38
  1266.4 18.5 %select_bitcast_fusion = f32[10,1,512,512]{2,3,0,1:T(8,128)} fusion(f32[10,512,512]{1,2,0:T(8,128)} %copy-done.3, f32[10,512,512]{1,2,0:T(8,128)} %copy.55, f32[10,512,512]{1,2,0:T(8,128)} %copy.47, f32[512]{0:T(512)S(1)} %gather_fusion.1, f32[512,512]{0,1:T(8,128)S(1)} %copy.56, f32[512]{0:T(512)S(1)} %gather_fusion, f32[512,512]{0,1:T(8,128)S(1)} %copy.52, ...), kind=kOutput, calls=%fused_computation.19 | convolution fusion | flops 2713190400 | bytes 49814020 | tf_op jit(solution)/shard_map/rab,cb->rac/dot_general | solution.py:38
  1284.9 16.2 %maximum_bitcast_fusion = f32[10,1,512,2,1,512]{2,5,0,3,4,1:T(8,128)} fusion(f32[10,1,512,512]{2,3,0,1:T(8,128)} %fusion.4, f32[10,1,512,512]{2,3,0,1:T(8,128)} %select_bitcast_fusion), kind=kLoop, calls=%fused_computation.8 | loop fusion | flops 5242880 | bytes 41943040 | tf_op jit(solution)/shard_map/broadcast_in_dim | solution.py:113
  1301.1 42.9 %copy.66 = f32[10,1,512,2,1,512]{5,4,3,2,1,0:T(1,128)} copy(f32[10,1,512,2,1,512]{2,5,0,3,4,1:T(8,128)} %maximum_bitcast_fusion) | data formatting | bytes 41943040 | tf_op jit(solution)/shard_map/broadcast_in_dim | solution.py:113
  (192 shorter events, 317.8 us)
Async XLA Ops:
  6.5 28.2 %copy-start = (f32[16,512]{1,0:T(8,128)S(1)}, f32[16,512]{1,0:T(8,128)}, u32[]{:S(2)}) copy-start(f32[16,512]{1,0:T(8,128)} %param.12) | copy-start | bytes 98308
  6.5 72.2 %all-reduce.13.cloned.1.call-start = ((), (), s32[]{:S(2)}) async-start(), calls=%async_computation.1 | async-start | bytes 4194304 | tf_op jit(solution)/shard_map/psum | solution.py:71
  24.5 214.4 %all-reduce.11.cloned.1.call-start = ((), (), s32[]{:S(2)}) async-start(), calls=%async_computation | async-start | bytes 8388608 | tf_op jit(solution)/shard_map/psum | solution.py:68
  33.4 275.0 %all-reduce.15.cloned.1.call-start = ((), (), s32[]{:S(2)}) async-start(), calls=%async_computation.2 | async-start | bytes 2097152 | tf_op jit(solution)/shard_map/psum | solution.py:11
  264.3 7.5 copy-start.2
  272.9 436.7 %all-reduce.17.cloned.1.call-start = ((), (), s32[]{:S(2)}) async-start(), calls=%async_computation.3 | async-start | bytes 10485760 | tf_op jit(solution)/shard_map/psum | solution.py:11
  310.1 87.8 %copy-start.13 = (s32[4]{0:T(128)S(1)}, s32[4]{0:T(128)}, u32[]{:S(2)}) copy-start(s32[4]{0:T(128)} %iota_multiply_fusion) | copy-start | bytes 52
  390.9 4.3 copy-start.6
  395.2 67.6 %slice-start = ((s8[10485760]{0:T(1024)(128)(4,1)}), s8[2097152]{0:T(1024)(128)(4,1)S(1)}, s32[]{:S(2)}) async-start(s8[10485760]{0:T(1024)(128)(4,1)} %bitcast.188), calls=%async_computation.8 | async-start | bytes 4194304
  449.6 13.3 slice-start.1
  454.0 6.3 copy-start.10
  454.0 8.9 slice-start.2
  508.5 11.3 copy-start.12
  527.7 221.7 %all-reduce.19.cloned.1.call-start = ((), (), s32[]{:S(2)}) async-start(), calls=%async_computation.4 | async-start | bytes 2097152 | tf_op jit(solution)/shard_map/psum | solution.py:11
  714.0 87.2 %all-reduce.21.cloned.1.call-start = ((), (), s32[]{:S(2)}) async-start(), calls=%async_computation.5 | async-start | bytes 2097152 | tf_op jit(solution)/shard_map/psum | solution.py:11
  759.3 3.8 copy-start.3
  764.3 444.1 %all-reduce.23.cloned.1.call-start = ((), (), s32[]{:S(2)}) async-start(), calls=%async_computation.6 | async-start | bytes 10485760 | tf_op jit(solution)/shard_map/psum | solution.py:11
  801.9 1.0 copy-start.7
  887.6 3.4 copy-start.5
  891.0 68.0 %slice-start.3 = ((s8[10485760]{0:T(1024)(128)(4,1)}), s8[2097152]{0:T(1024)(128)(4,1)S(1)}, s32[]{:S(2)}) async-start(s8[10485760]{0:T(1024)(128)(4,1)} %bitcast.194), calls=%async_computation.11 | async-start | bytes 4194304
  945.7 13.3 slice-start.4
  950.1 6.3 copy-start.11
  950.1 8.9 slice-start.5
  1024.0 224.1 %all-reduce.25.cloned.1.call-start = ((), (), s32[]{:S(2)}) async-start(), calls=%async_computation.7 | async-start | bytes 2097152 | tf_op jit(solution)/shard_map/psum | solution.py:11
  1031.6 181.0 %copy-start.8 = (bf16[2,512,512]{1,2,0:T(8,128)(2,1)S(1)}, bf16[2,512,512]{1,2,0:T(8,128)(2,1)}, u32[]{:S(2)}) copy-start(bf16[2,512,512]{1,2,0:T(8,128)(2,1)} %all-reduce.19.cloned.1.call-done) | copy-start | bytes 3145732
  1212.6 8.4 copy-start.4
  1248.0 18.4 %copy-start.9 = (bf16[2,512,512]{1,2,0:T(8,128)(2,1)S(1)}, bf16[2,512,512]{1,2,0:T(8,128)(2,1)}, u32[]{:S(2)}) copy-start(bf16[2,512,512]{1,2,0:T(8,128)(2,1)} %all-reduce.25.cloned.1.call-done) | copy-start | bytes 3145732
  1301.0 42.9 %copy-start.1 = (f32[16,512]{1,0:T(8,128)S(1)}, f32[16,512]{1,0:T(8,128)}, u32[]{:S(2)}) copy-start(f32[16,512]{1,0:T(8,128)} %param.12) | copy-start | bytes 98308
Sparse Core Ops, SparseCore 0:
  24.6 54.0 all-reduce.12
  82.4 156.4 all-reduce.10
  273.1 35.2 all-reduce.14
  527.8 181.7 all-reduce.16
  714.1 35.2 all-reduce.18
  764.4 36.7 all-reduce.20
  1024.1 184.2 all-reduce.22
  1212.7 35.2 all-reduce.24
where the time goes:
time: 1360 us; the launch traced here: 1350 us
  waiting for transfers between devices  641 us (47%)
  other arithmetic  318 us (23%)
  local copies, waits for them, and re-layouts  193 us (14%)
  matrix products  178 us (13%)
  between operations  21.1 us (2%)
    psum x6, waiting for transfers between devices, spread(): return lax.psum(jnp.where(mine, value, jnp.zeros_like(value)), axis)  456 us
    another operation x29, other arithmetic, factor_panel(): factor = jnp.linalg.cholesky(pivot_tile)  159 us
    psum x1, waiting for transfers between devices, on_device(): partial_rows = lax.psum(row_terms[:kept_rows], 'pcol')  157 us
    another operation x7, other arithmetic, factor_panel(): lax.linalg.triangular_solve(factor, column.reshape(-1, extent), left_side...  94.9 us
    another operation x14, matrix products, factor_panel(): lax.linalg.triangular_solve(factor, column.reshape(-1, extent), left_side...  85.9 us
    dot_general x4, matrix products, trailing(): jnp.einsum('rab,cb->rac', received, other_rows, preferred_element_type=jn...  55.1 us
    another operation x29, local copies, waits for them, and re-layouts, factor_panel(): lax.linalg.triangular_solve(factor, column.reshape(-1, extent), left_side...  46.2 us
    broadcast_in_dim x1, local copies, waits for them, and re-layouts, on_device(): return stacked.transpose(0, 2, 1, 3)[:, None, :, :, None, :]  42.9 us
  transfers between devices with their start and end apart: 8, of which 8 were waited for; matrix products, arithmetic and copies ran while one was open for 6% of the time, Pallas kernels for 0%

commit v1 on v0

--- a/solution.py
+++ b/solution.py
@@ -65,7 +65,7 @@
         "crtak,crtbk->tab", right_factor, right_factor, preferred_element_type=jnp.float32
     )
     kept_rows = cols_here * pcol_count // prow_count
-    partial_rows = lax.psum(row_terms[:kept_rows], "pcol")
+    partial_rows = jnp.sum(lax.all_gather(row_terms[:kept_rows], "pcol"), axis=0)
     spare_rows = jnp.zeros((rows_here - kept_rows, extent, extent), jnp.float32)
     row_sums = jnp.concatenate([partial_rows, spare_rows], axis=0)
     column_sums = lax.psum(column_terms, "prow")

time: 1360 us -> 1820 us (1.34)
  waiting for transfers between devices: 641 us -> 1080 us
    all_gather x0 -> x1, waiting for transfers between devices: none -> 593 us  [on_device(): lax.all_gather(row_terms[:kept_rows], 'pcol')]
    psum x1 -> x0, waiting for transfers between devices: 157 us -> none  [on_device(): partial_rows = lax.psum(row_terms[:kept_rows], 'pcol')]
  transfers between devices with their start and end apart: 8 -> 8, of which waited for: 8 -> 8; matrix products, arithmetic and copies ran while one was open for 6% -> 5% of each run, Pallas kernels for 0% -> 0%
where the time goes in v1:
time: 1820 us; the launch traced here: 1800 us
  waiting for transfers between devices  1080 us (59%)
  other arithmetic  333 us (18%)
  local copies, waits for them, and re-layouts  193 us (11%)
  matrix products  179 us (10%)
  between operations  22.5 us (1%)
    all_gather x1, waiting for transfers between devices, on_device(): lax.all_gather(row_terms[:kept_rows], 'pcol')  593 us
    psum x6, waiting for transfers between devices, spread(): return lax.psum(jnp.where(mine, value, jnp.zeros_like(value)), axis)  456 us
    another operation x29, other arithmetic, factor_panel(): factor = jnp.linalg.cholesky(pivot_tile)  159 us
    another operation x7, other arithmetic, factor_panel(): lax.linalg.triangular_solve(factor, column.reshape(-1, extent), left_side...  95.1 us
    another operation x14, matrix products, factor_panel(): lax.linalg.triangular_solve(factor, column.reshape(-1, extent), left_side...  85.9 us
    dot_general x4, matrix products, trailing(): jnp.einsum('rab,cb->rac', received, other_rows, preferred_element_type=jn...  55.1 us
    another operation x29, local copies, waits for them, and re-layouts, factor_panel(): lax.linalg.triangular_solve(factor, column.reshape(-1, extent), left_side...  46 us
    broadcast_in_dim x1, local copies, waits for them, and re-layouts, on_device(): return stacked.transpose(0, 2, 1, 3)[:, None, :, :, None, :]  42.9 us
  transfers between devices with their start and end apart: 8, of which 8 were waited for; matrix products, arithmetic and copies ran while one was open for 5% of the time, Pallas kernels for 0%

profile of v1, /device:TPU:0, one launch (start us, length us, event | category | flops | bytes accessed | tf_op | source)
XLA Modules:
  0.0 1803.4 jit_solution(8560820120586927948)
XLA Ops:
  37.1 15.2 convolution_bitcast_fusion
  52.3 27.2 %all-reduce.10.cloned.1.call-done = f32[2,512,512]{2,1,0:T(8,128)} async-done(((f32[2,512,512]{2,1,0:T(8,128)}), f32[2,512,512]{2,1,0:T(8,128)}) %all-reduce.10.cloned.1.call-update) | async-done | bytes 2097168 | tf_op jit(solution)/shard_map/psum | solution.py:71
  82.4 592.6 %all-gather.3.cloned.1.call-done = f32[32,512,512]{2,1,0:T(8,128)} async-done(((f32[4,512,512]{2,1,0:T(8,128)}), f32[32,512,512]{2,1,0:T(8,128)}) %all-gather.3.cloned.1.call-update) | async-done | bytes 33554448 | tf_op jit(solution)/shard_map/all_gather | solution.py:68
  675.0 15.1 reduce_sum.9
  702.8 12.6 copy_add_fusion
  733.2 11.6 copy.73
  744.9 15.6 all-reduce.12.cloned.1.call-done
  763.7 11.7 cholesky.286
  786.0 11.7 cholesky.305
  808.4 11.7 cholesky.326
  831.2 11.7 cholesky.343
  850.0 11.9 while.4
  861.9 39.9 %custom-call.34 = f32[4,128,128]{1,2,0:T(8,128)} custom-call(f32[4,128,128]{2,1,0:T(8,128)S(1)} %get-tuple-element.22), custom_call_target="InvertDiagBlocksLowerTriangular" | custom-call | tf_op jit(solution)/shard_map/triangular_solve/custom-call.3 | solution.py:20
  927.7 14.6 fusion.20
  949.4 11.4 copy.74
  980.2 181.6 %all-reduce.14.cloned.1.call-done = bf16[10,512,512]{1,2,0:T(8,128)(2,1)} async-done(((bf16[10,512,512]{1,2,0:T(8,128)(2,1)}), bf16[10,512,512]{1,2,0:T(8,128)(2,1)}) %all-reduce.14.cloned.1.call-update) | async-done | bytes 5242896 | tf_op jit(solution)/shard_map/psum | solution.py:11
  1166.2 35.4 %all-reduce.16.cloned.1.call-done = bf16[2,512,512]{1,2,0:T(8,128)(2,1)} async-done(((bf16[2,512,512]{1,2,0:T(8,128)(2,1)}), bf16[2,512,512]{1,2,0:T(8,128)(2,1)}) %all-reduce.16.cloned.1.call-update) | async-done | bytes 1048592 | tf_op jit(solution)/shard_map/psum | solution.py:11
  1216.5 11.5 copy.81
  1227.9 25.4 %all-reduce.18.cloned.1.call-done = f32[512,512]{0,1:T(8,128)} async-done(((f32[512,512]{0,1:T(8,128)}), f32[512,512]{0,1:T(8,128)}) %all-reduce.18.cloned.1.call-update) | async-done | bytes 1048592 | tf_op jit(solution)/shard_map/psum | solution.py:11
  1255.0 11.7 cholesky.358
  1279.3 11.7 cholesky.377
  1304.1 11.7 cholesky.398
  1327.8 11.7 cholesky.415
  1357.5 39.9 %custom-call.38 = f32[4,128,128]{1,2,0:T(8,128)} custom-call(f32[4,128,128]{2,1,0:T(8,128)S(1)} %get-tuple-element.23), custom_call_target="InvertDiagBlocksLowerTriangular" | custom-call | tf_op jit(solution)/shard_map/triangular_solve/custom-call.3 | solution.py:20
  1423.5 14.4 fusion.17
  1456.5 11.5 copy.83
  1484.4 175.6 %all-reduce.20.cloned.1.call-done = bf16[10,512,512]{1,2,0:T(8,128)(2,1)} async-done(((bf16[10,512,512]{1,2,0:T(8,128)(2,1)}), bf16[10,512,512]{1,2,0:T(8,128)(2,1)}) %all-reduce.20.cloned.1.call-update) | async-done | bytes 5242896 | tf_op jit(solution)/shard_map/psum | solution.py:11
  1677.7 22.1 %all-reduce.22.cloned.1.call-done = bf16[2,512,512]{1,2,0:T(8,128)(2,1)} async-done(((bf16[2,512,512]{1,2,0:T(8,128)(2,1)}), bf16[2,512,512]{1,2,0:T(8,128)(2,1)}) %all-reduce.22.cloned.1.call-update) | async-done | bytes 1048592 | tf_op jit(solution)/shard_map/psum | solution.py:11
  1699.7 18.4 %fusion.4 = f32[10,1,512,512]{2,3,0,1:T(8,128)} fusion(f32[10,512,512]{1,2,0:T(8,128)} %fusion.47, f32[10,2,512,512]{2,3,1,0:T(8,128)} %copy-done.2, pred[10]{0:T(512)(128)(4,1)S(1)} %get-tuple-element.76, pred[]{:T(512)S(6)} %lt.48, bf16[10,512,512]{1,2,0:T(8,128)(2,1)} %all-reduce.20.cloned.1.call-done, bf16[2,512,512]{1,2,0:T(8,128)(2,1)} %all-reduce.22.cloned.1.call-done), kind=kOutput, calls=%fused_computation.15 | convolution fusion | flops 2694840320 | bytes 37224460 | tf_op jit(solution)/shard_map/rab,cb->rac/dot_general | solution.py:38
  1718.1 18.5 %select_bitcast_fusion = f32[10,1,512,512]{2,3,0,1:T(8,128)} fusion(f32[10,512,512]{1,2,0:T(8,128)} %copy-done.3, f32[10,512,512]{1,2,0:T(8,128)} %copy.83, f32[10,512,512]{1,2,0:T(8,128)} %copy.75, f32[512]{0:T(512)S(1)} %gather_fusion.1, f32[512,512]{0,1:T(8,128)S(1)} %copy.84, f32[512]{0:T(512)S(1)} %gather_fusion, f32[512,512]{0,1:T(8,128)S(1)} %copy.80, ...), kind=kOutput, calls=%fused_computation.19 | convolution fusion | flops 2713190400 | bytes 49814020 | tf_op jit(solution)/shard_map/rab,cb->rac/dot_general | solution.py:38
  1736.6 16.2 maximum_bitcast_fusion
  1752.7 42.9 %copy.94 = f32[10,1,512,2,1,512]{5,4,3,2,1,0:T(1,128)} copy(f32[10,1,512,2,1,512]{2,5,0,3,4,1:T(8,128)} %maximum_bitcast_fusion) | data formatting | bytes 41943040 | tf_op jit(solution)/shard_map/broadcast_in_dim | solution.py:113
  (195 shorter events, 329.2 us)
Async XLA Ops:
  7.4 28.0 %copy-start = (f32[16,512]{1,0:T(8,128)S(1)}, f32[16,512]{1,0:T(8,128)}, u32[]{:S(2)}) copy-start(f32[16,512]{1,0:T(8,128)} %param.12) | copy-start | bytes 98308
  7.4 72.2 %all-reduce.10.cloned.1.call-start = ((), (), s32[]{:S(2)}) async-start(), calls=%async_computation | async-start | bytes 4194304 | tf_op jit(solution)/shard_map/psum | solution.py:71
  25.3 649.7 %all-gather.3.cloned.1.call-start = ((), (), s32[]{:S(2)}) async-start(), calls=%async_computation.7 | async-start | bytes 37748736 | tf_op jit(solution)/shard_map/all_gather | solution.py:68
  34.5 726.0 %all-reduce.12.cloned.1.call-start = ((), (), s32[]{:S(2)}) async-start(), calls=%async_computation.1 | async-start | bytes 2097152 | tf_op jit(solution)/shard_map/psum | solution.py:11
  34.6 0.8 copy-start.12
  715.4 7.5 copy-start.2
  724.1 437.7 %all-reduce.14.cloned.1.call-start = ((), (), s32[]{:S(2)}) async-start(), calls=%async_computation.2 | async-start | bytes 10485760 | tf_op jit(solution)/shard_map/psum | solution.py:11
  762.2 87.8 %copy-start.14 = (s32[4]{0:T(128)S(1)}, s32[4]{0:T(128)}, u32[]{:S(2)}) copy-start(s32[4]{0:T(128)} %iota_multiply_fusion) | copy-start | bytes 52
  843.0 4.4 copy-start.6
  847.4 67.7 %slice-start = ((s8[10485760]{0:T(1024)(128)(4,1)}), s8[2097152]{0:T(1024)(128)(4,1)S(1)}, s32[]{:S(2)}) async-start(s8[10485760]{0:T(1024)(128)(4,1)} %bitcast.189), calls=%async_computation.8 | async-start | bytes 4194304
  901.9 13.3 slice-start.1
  906.3 6.3 copy-start.10
  906.3 8.9 slice-start.2
  980.0 221.5 %all-reduce.16.cloned.1.call-start = ((), (), s32[]{:S(2)}) async-start(), calls=%async_computation.3 | async-start | bytes 2097152 | tf_op jit(solution)/shard_map/psum | solution.py:11
  1166.1 87.2 %all-reduce.18.cloned.1.call-start = ((), (), s32[]{:S(2)}) async-start(), calls=%async_computation.4 | async-start | bytes 2097152 | tf_op jit(solution)/shard_map/psum | solution.py:11
  1211.4 3.8 copy-start.3
  1216.4 443.6 %all-reduce.20.cloned.1.call-start = ((), (), s32[]{:S(2)}) async-start(), calls=%async_computation.5 | async-start | bytes 10485760 | tf_op jit(solution)/shard_map/psum | solution.py:11
  1254.0 1.0 copy-start.7
  1339.7 3.4 copy-start.5
  1343.1 67.6 %slice-start.3 = ((s8[10485760]{0:T(1024)(128)(4,1)}), s8[2097152]{0:T(1024)(128)(4,1)S(1)}, s32[]{:S(2)}) async-start(s8[10485760]{0:T(1024)(128)(4,1)} %bitcast.195), calls=%async_computation.11 | async-start | bytes 4194304
  1397.5 13.2 slice-start.4
  1401.9 6.3 copy-start.11
  1401.9 8.8 slice-start.5
  1475.8 0.6 copy-start.13
  1475.8 223.9 %all-reduce.22.cloned.1.call-start = ((), (), s32[]{:S(2)}) async-start(), calls=%async_computation.6 | async-start | bytes 2097152 | tf_op jit(solution)/shard_map/psum | solution.py:11
  1483.9 180.3 %copy-start.8 = (bf16[2,512,512]{1,2,0:T(8,128)(2,1)S(1)}, bf16[2,512,512]{1,2,0:T(8,128)(2,1)}, u32[]{:S(2)}) copy-start(bf16[2,512,512]{1,2,0:T(8,128)(2,1)} %all-reduce.16.cloned.1.call-done) | copy-start | bytes 3145732
  1664.3 8.4 copy-start.4
  1699.7 18.4 %copy-start.9 = (bf16[2,512,512]{1,2,0:T(8,128)(2,1)S(1)}, bf16[2,512,512]{1,2,0:T(8,128)(2,1)}, u32[]{:S(2)}) copy-start(bf16[2,512,512]{1,2,0:T(8,128)(2,1)} %all-reduce.22.cloned.1.call-done) | copy-start | bytes 3145732
  1752.7 42.9 %copy-start.1 = (f32[16,512]{1,0:T(8,128)S(1)}, f32[16,512]{1,0:T(8,128)}, u32[]{:S(2)}) copy-start(f32[16,512]{1,0:T(8,128)} %param.12) | copy-start | bytes 98308
Sparse Core Ops, SparseCore 0:
  25.4 54.0 all-reduce.9
  724.2 36.2 all-reduce.11
  1166.2 35.2 all-reduce.15
  1216.5 36.7 all-reduce.17
  1664.4 35.2 all-reduce.21
Sparse Core Ops, SparseCore 1:
  34.6 640.4 all-gather.2
  980.1 181.6 all-reduce.13
  1475.9 184.1 all-reduce.19
